TPU v7x, 256 devices: a whole 4x4x8 slice. The times are simulated.
256 devices in a mesh: clu: 128 (over z, y, x), rep: 2 (over core).
Axes of the slice: x: 4, y: 4, z: 8, core: 2. Of those that a mesh axis runs over, the one named last changes fastest.
Arguments:
- current: float32 [256, 2, 2, 2048], P('clu', None, 'rep'), may hold values from -6 to 6
- factors: float32 [512, 2, 2, 128, 2048], P(('clu', 'rep')), may hold values from -0.0625 to 0.0625
- ranks: int32 [512], P(('clu', 'rep')), may hold values from 8 to 40
- pair_clusters: int32 [512, 2], replicated, may hold values from 0 to 255, as said below
Outputs:
- field: float32 [256, 2, 2, 2048], P('clu', None, 'rep')
Inputs may be any that keep to these rules, and one draw needn't show every extreme that they name: `pair_clusters`: the 4 cluster ids of the pairs of one device (pairs in blocks of 2 in order) are all different.
All inputs are finite; a program needn't handle non-finite values.
Results may differ from a plain program's by a relative error of at most 0.0003.
Values sent between devices are 32-bit elements; how exact they have to be, the bound alone decides.
A program may use at most 128 MiB of HBM per device.

v0:
```python
import jax
import jax.numpy as jnp
from jax import lax
from jax.sharding import PartitionSpec as P


def project_rows(factor, vector, rank_mask):
    high = lax.Precision.HIGHEST
    real_part = jnp.einsum("prc,pkc->prk", factor[:, 0], vector[:, 0], precision=high) - jnp.einsum(
        "prc,pkc->prk", factor[:, 1], vector[:, 1], precision=high
    )
    imag_part = jnp.einsum("prc,pkc->prk", factor[:, 0], vector[:, 1], precision=high) + jnp.einsum(
        "prc,pkc->prk", factor[:, 1], vector[:, 0], precision=high
    )
    return jnp.stack((real_part, imag_part), axis=1) * rank_mask[:, None, :, None]


def expand_rows(factor, projected):
    high = lax.Precision.HIGHEST
    real_part = jnp.einsum(
        "prc,prk->pkc", factor[:, 0], projected[:, 0], precision=high
    ) - jnp.einsum("prc,prk->pkc", factor[:, 1], projected[:, 1], precision=high)
    imag_part = jnp.einsum(
        "prc,prk->pkc", factor[:, 0], projected[:, 1], precision=high
    ) + jnp.einsum("prc,prk->pkc", factor[:, 1], projected[:, 0], precision=high)
    return jnp.stack((real_part, imag_part), axis=1)


def local(current, factors, ranks, pair_clusters):
    high = lax.Precision.HIGHEST
    clu_count = current.shape[0]
    excitations = current.shape[2] * lax.axis_size("rep")
    unknowns = current.shape[3]
    pair_count = factors.shape[0]
    end_count = 2 * pair_count
    n_rep = lax.axis_size("rep")
    block_index = lax.axis_index("clu") * n_rep + lax.axis_index("rep")
    row_width = 2 * excitations * unknowns
    whole_rhs = lax.all_gather(current, "rep", axis=2, tiled=True)
    flattened = whole_rhs.reshape(clu_count, row_width)
    my_pairs = lax.dynamic_slice_in_dim(pair_clusters, block_index * pair_count, pair_count, 0)
    my_ids = my_pairs.reshape(end_count)
    everything = lax.all_gather(flattened, "clu", axis=0, tiled=True)
    pieces = jnp.take(everything, my_ids, axis=0)
    pieces = pieces.reshape(pair_count, 2, 2, excitations, unknowns)
    left_factor = factors[:, 0]
    right_factor = factors[:, 1]
    rank_mask = (jnp.arange(factors.shape[3], dtype=jnp.int32)[None, :] < ranks[:, None]).astype(
        factors.dtype
    )
    row_terms = expand_rows(left_factor, project_rows(right_factor, pieces[:, 1], rank_mask))
    col_terms = expand_rows(right_factor, project_rows(left_factor, pieces[:, 0], rank_mask))
    contributions = jnp.stack((row_terms, col_terms), axis=1).reshape(end_count, row_width)
    positions = jnp.arange(clu_count * lax.axis_size("clu"), dtype=jnp.int32)
    placer = (positions[:, None] == my_ids[None, :]).astype(jnp.float32)
    summed = lax.psum_scatter(
        jnp.dot(placer, contributions, precision=high), "clu", scatter_dimension=0, tiled=True
    )
    summed = summed.reshape(clu_count, 2, excitations, unknowns)
    return lax.psum_scatter(summed, "rep", scatter_dimension=2, tiled=True)


def solution(mesh):
    placed = (
        P("clu", None, "rep", None),
        P(("clu", "rep"), None, None, None, None),
        P(("clu", "rep")),
        P(),
    )
    return jax.shard_map(
        local, mesh=mesh, in_specs=placed, out_specs=P("clu", None, "rep", None), check_vma=False
    )
```

profile of v0, /device:TPU:1, one launch (start us, length us, event | category | flops | bytes accessed | tf_op | source)
XLA Modules:
  0.0 483.8 jit_solution(11641108925071819487)
XLA Ops:
  6.5 0.8 copy.25
  7.3 4.7 all_gather.6
  12.1 0.1 copy.26
  12.1 0.7 reshape.86
  12.8 0.0 all-gather.3.cloned.1.call-update
  12.9 0.0 all-reduce.5.cloned.1.call-start
  12.9 0.8 compare_and_fusion
  13.7 0.1 copy.24
  13.8 0.1 reshape.75
  13.9 0.1 eq.16
  13.9 0.7 compare_convert_fusion
  14.7 4.0 fusion.27
  18.7 3.8 copy_bitcast_fusion
  22.5 113.4 %all-gather.3.cloned.1.call-done = f32[128,2,8192]{2,1,0:T(2,128)} async-done(((f32[1,2,8192]{2,1,0:T(2,128)}), f32[128,2,8192]{2,1,0:T(2,128)}) %all-gather.3.cloned.1.call-update) | async-done | bytes 8388624 | tf_op jit(solution)/shard_map/all_gather | solution.py:43
  135.9 10.8 %reshape.87 = f32[256,8192]{1,0:T(8,128)} reshape(f32[128,2,8192]{2,1,0:T(2,128)} %all-gather.3.cloned.1.call-done) | data formatting | bytes 16777216
  146.8 4.0 gather_fusion
  150.9 0.1 gather.7
  151.0 0.1 copy_select_fusion
  151.2 3.5 fusion.11
  154.7 3.4 fusion.10
  158.1 1.8 fusion.7
  160.0 1.8 fusion.6
  161.8 1.8 fusion.17
  163.6 1.8 fusion.19
  165.5 1.8 fusion.21
  167.3 1.8 fusion.23
  169.2 1.3 fusion.13
  170.5 1.1 fusion.12
  171.6 1.1 fusion.5
  172.7 1.1 fusion.4
  173.8 1.1 fusion.3
  174.9 1.1 fusion.2
  176.0 1.1 fusion.1
  177.1 1.1 fusion
  178.3 0.1 pad_maximum_fusion
  178.4 0.1 reshape.76
  178.5 5.6 %fusion.24 = f32[256,8192]{1,0:T(8,128)} fusion(f32[4,8192]{1,0:T(4,128)S(1)} %reshape.76, s32[4]{0:T(128)S(1)} %eq.16), kind=kOutput, calls=%fused_computation.38 | convolution fusion | flops 100664320 | bytes 8519696 | tf_op jit(solution)/shard_map/dot_general | solution.py:57
  184.1 0.0 all-reduce.7.cloned.1.call-start
  184.2 0.6 copy-done.3
  184.8 0.6 dynamic-slice
  186.0 258.2 %all-reduce.5.cloned.1.call-done = f32[256,8192]{1,0:T(8,128)} async-done(((f32[256,8192]{1,0:T(8,128)}), f32[256,8192]{1,0:T(8,128)}) %all-reduce.5.cloned.1.call-update) | async-done | bytes 8388624
  444.2 1.0 constant_dynamic-slice_fusion.1
  445.2 0.1 reshape.77
  445.3 0.7 copy.32
  446.0 0.6 dynamic-slice.2
  446.6 28.6 %all-reduce.7.cloned.1.call-done = f32[2,2,2,2048]{3,1,0,2:T(2,128)} async-done(((f32[2,2,2,2048]{3,1,0,2:T(2,128)}), f32[2,2,2,2048]{3,1,0,2:T(2,128)}) %all-reduce.7.cloned.1.call-update) | async-done | bytes 65552
  475.2 1.4 constant_dynamic-slice_fusion
  476.6 0.6 copy.33
  (17 shorter events, 0.2 us)
Async XLA Ops:
  6.5 129.4 %all-gather.3.cloned.1.call-start = ((), (), s32[]{:S(2)}) async-start(), calls=%async_computation | async-start | bytes 8454144 | tf_op jit(solution)/shard_map/all_gather | solution.py:43
  12.9 431.4 %all-reduce.5.cloned.1.call-start = ((), (), s32[]{:S(2)}) async-start(), calls=%async_computation.1 | async-start | bytes 16777216
  151.0 7.1 %copy-start = (f32[2,2,128,2048]{3,2,0,1:T(8,128)S(1)}, f32[2,2,128,2048]{3,2,0,1:T(8,128)}, u32[]{:S(2)}) copy-start(f32[2,2,128,2048]{3,2,0,1:T(8,128)} %get-tuple-element.14) | copy-start | bytes 12582916
  151.1 10.7 %copy-start.1 = (f32[2,2,128,2048]{3,2,0,1:T(8,128)S(1)}, f32[2,2,128,2048]{3,2,0,1:T(8,128)}, u32[]{:S(2)}) copy-start(f32[2,2,128,2048]{3,2,0,1:T(8,128)} %get-tuple-element.13) | copy-start | bytes 12582916
  184.1 0.7 copy-start.3
  184.1 261.9 %copy-start.2 = (u32[256]{0:T(256)S(1)}, u32[256]{0:T(256)}, u32[]{:S(2)}) copy-start(u32[256]{0:T(256)} %constant.38) | copy-start | bytes 3076
  184.1 291.0 %all-reduce.7.cloned.1.call-start = ((), (), s32[]{:S(2)}) async-start(), calls=%async_computation.2 | async-start | bytes 131072
Sparse Core Ops, SparseCore 0:
  13.0 122.9 all-gather.2
  184.3 259.8 all-reduce.4
  446.9 28.1 all-reduce.6
where the time goes:
time: 484 us
  waiting for transfers between devices  400 us (83%)
  matrix products  32.6 us (7%)
  local copies, waits for them, and re-layouts  30.4 us (6%)
  between operations  13.9 us (3%)
    unnamed x5, waiting for transfers between devices  287 us
    all_gather x1, waiting for transfers between devices, local(): everything = lax.all_gather(flattened, 'clu', axis=0, tiled=True)  113 us
    unnamed x15, local copies, waits for them, and re-layouts  16.5 us
  transfers between devices with their start and end apart: 3, of which 3 were waited for; matrix products, arithmetic and copies ran while one was open for 2% of the time, Pallas kernels for 0%

commit v1 on v0

v1 whole, which is shorter than its diff:
```python
import functools

import jax
import jax.numpy as jnp
from jax import lax
from jax.experimental import pallas as pl
from jax.experimental.pallas import tpu as pltpu
from jax.sharding import PartitionSpec as P

MESH = pl.DeviceIdType.MESH
LANES = 128
RANK_ROWS = 64
F32, BF16 = jnp.float32, jnp.bfloat16


def near_last(count):
    return sorted(range(1, count), key=lambda d: (-min(d, count - d), d))


def kernel(
    dims, ids_ref, ranks_ref, cur_ref, fac_ref, out_ref,
    pool, packed, refs, vecs, split, vec8, contrib, items, sums, terms, partial, parts, fac_buf,
    z_send, z_recv, d_send, d_recv, s_send, s_recv, c_send, c_recv, r_send, r_recv, y_send, y_recv, fac_sem,
):
    lz, ly, lx = dims
    side = (ly, lx)
    cross = (lx, ly)
    rows = cur_ref.shape[2]
    clu, rep = lax.axis_index("clu"), lax.axis_index("rep")
    other = 1 - rep
    mx, my, mz = lax.rem(clu, lx), lax.rem(lax.div(clu, lx), ly), lax.div(clu, lx * ly)

    def chip(dx=0, dy=0, dz=0):
        x, y, z = lax.rem(mx + dx, lx), lax.rem(my + dy, ly), lax.rem(mz + dz, lz)
        return (z * ly + y) * lx + x

    def along_side(half, d):
        return chip(dy=d % ly) if half == 0 else chip(dx=d % lx)

    def along_cross(half, d):
        return chip(dx=d % lx) if half == 0 else chip(dy=d % ly)

    def ref_id(at, s):
        return ids_ref[s % 2, at * 4 + s // 2]

    def place(cid):
        owner = lax.div(cid, 2)
        x, y, z = lax.rem(owner, lx), lax.rem(lax.div(owner, lx), ly), lax.div(owner, lx * ly)
        return x, y, z, lax.rem(cid, 2)

    def remote(src, dst, ssem, rsem, to, core):
        return pltpu.make_async_remote_copy(
            src_ref=src, dst_ref=dst, send_sem=ssem, recv_sem=rsem, device_id=(to, core), device_id_type=MESH
        )

    fac_copies = []
    for p in range(2):
        for e in range(2):
            copy = pltpu.make_async_copy(
                fac_ref.at[p, e, :, pl.ds(0, RANK_ROWS), :], fac_buf.at[p * 2 + e], fac_sem.at[p * 2 + e]
            )
            copy.start()
            fac_copies.append(copy)

    barrier = pltpu.get_barrier_semaphore()
    peers = [(clu, other)]
    peers += [(chip(dz=d), rep) for d in range(1, lz)]
    for half in range(2):
        for d in range(1, cross[half]):
            peers += [(along_cross(half, d), rep), (along_cross(half, d), other)]
    for peer in peers:
        pl.semaphore_signal(barrier, inc=1, device_id=peer, device_id_type=MESH)
    for half in range(2):
        for cl in range(2):
            pool[half, cl] = cur_ref[cl, half]
    pl.semaphore_wait(barrier, len(peers))

    z_copies = {}
    for d in near_last(lz):
        z_copies[d] = remote(
            pool.at[:, pl.ds(0, 2)], pool.at[:, pl.ds(2 * d, 2)], z_send.at[d], z_recv.at[d], chip(dz=d), rep
        )
        z_copies[d].start()

    def forward(dz):
        for half in range(2):
            for d in near_last(side[half]):
                remote(
                    pool.at[half, pl.ds(2 * dz, 2)], pool.at[half, pl.ds((d * lz + dz) * 2, 2)],
                    d_send.at[half, d], d_recv.at[half, d], along_side(half, d), rep,
                ).start()

    def split_factor(f):
        fac_copies[f].wait()
        for part in range(2):
            value = fac_buf[f, part]
            high = value.astype(BF16)
            split[f, pl.ds(part * RANK_ROWS, RANK_ROWS), :] = high
            split[f, pl.ds((2 + part) * RANK_ROWS, RANK_ROWS), :] = (value - high.astype(F32)).astype(BF16)

    forward(0)
    split_factor(0)
    split_factor(1)
    arrival = near_last(lz)[::-1]
    for n, dz in enumerate(arrival):
        z_copies[dz].wait_recv()
        forward(dz)
        if n == len(arrival) // 2:
            split_factor(2)
    split_factor(3)
    for half in range(2):
        for d in range(1, side[half]):
            whole = pool.at[half, pl.ds(d * lz * 2, lz * 2)]
            pltpu.make_async_copy(whole, whole, d_recv.at[half, d]).wait()

    s_copies = []
    for half in range(2):
        for d in near_last(cross[half]) + [0]:
            to = along_cross(half, d)
            for s in range(8):
                x, y, z, cl = place(ref_id(to, s))
                shift = lax.rem((my - y if half == 0 else mx - x) + side[half], side[half])
                slot = (shift * lz + lax.rem(mz - z + lz, lz)) * 2 + cl
                packed[half, d, s // 4, s % 4] = pool[half, slot]
            for q, core in ((0, rep), (1, other)):
                if d == 0 and q == 0:
                    refs[half, 0, rep] = packed[half, 0, rep]
                    continue
                copy = remote(
                    packed.at[half, d, core], refs.at[half, d, rep],
                    s_send.at[half, d, q], s_recv.at[half, d, q], to, core,
                )
                copy.start()
                s_copies.append(copy)

    lane = lax.broadcasted_iota(jnp.int32, (8, LANES), 1)
    placers = []
    for half in range(2):
        target = jnp.full((8, LANES), -1, jnp.int32)
        for d in range(cross[half]):
            source = along_cross(half, cross[half] - d)
            for s in range(8):
                x, y, z, cl = place(ref_id(source, s))
                mine = (x == mx) if half == 0 else (y == my)
                shift = lax.rem((y - my if half == 0 else x - mx) + side[half], side[half])
                slot = (shift * lz + lax.rem(z - mz + lz, lz)) * 2 + cl
                slot = jnp.where(mine, slot, -1)
                at = d * 8 + s
                target = jnp.where((lane == at) | (lane == at + 8 * cross[half]), slot, target)
        slots = side[half] * lz * 2
        wide = jnp.concatenate([target] * (slots // 8), axis=0)[:, : 16 * cross[half]]
        placers.append(
            jnp.where(lax.broadcasted_iota(jnp.int32, wide.shape, 0) == wide, 1.0, 0.0).astype(BF16)
        )

    for copy in s_copies:
        copy.wait_recv()

    row = lax.broadcasted_iota(jnp.int32, (8, LANES), 0)
    col = lax.broadcasted_iota(jnp.int32, (8, LANES), 1)
    first = row < 4
    sign = jnp.where(lax.rem(row, 4) < 2, -1.0, 1.0).astype(F32)
    for s in range(4):
        x, y, z, cl = place(ids_ref[s % 2, clu * 4 + rep * 2 + s // 2])
        dx, dy = lax.rem(mx - x + lx, lx), lax.rem(my - y + ly, ly)
        for k in range(2):
            for half, d in ((0, dx), (1, dy)):
                value = refs[half, d, k, s]
                vecs[s, pl.ds((half * 2 + k) * rows, rows), :] = value
                vecs[s, pl.ds((4 + half * 2 + k) * rows, rows), :] = value
    for s in range(4):
        p, e = s // 2, s % 2
        for j in range(rows):
            value = vecs[s, pl.ds(j, 8, stride=rows), :]
            high = value.astype(BF16).astype(F32)
            vec8[s, :, pl.ds(j * LANES, LANES)] = jnp.where(first, high, value - high).astype(BF16)
        got = lax.dot_general(
            vec8[s], split[p * 2 + e], (((1,), (1,)), ((), ())), preferred_element_type=F32
        )
        both = got[:, :LANES] + got[:, LANES:]
        both = both + pltpu.roll(both, 4, 0)
        t = both + sign * pltpu.roll(pltpu.roll(both, RANK_ROWS, 1), 2, 0)
        t = jnp.where(col < jnp.minimum(ranks_ref[p], RANK_ROWS), t, 0.0)
        t = t + pltpu.roll(sign * pltpu.roll(t, 2, 0), RANK_ROWS, 1)
        high = t.astype(BF16).astype(F32)
        t = jnp.where(first, high, t - high).astype(BF16)
        t = jnp.concatenate([t, t], axis=1)
        target = p * 2 + 1 - e
        for j in range(rows // 2):
            out = jnp.dot(
                t, split[p * 2 + 1 - e, :, pl.ds(j * 2 * LANES, 2 * LANES)], preferred_element_type=F32
            )
            for i in range(2):
                block = out[:, i * LANES : (i + 1) * LANES]
                block = block + pltpu.roll(block, 4, 0)
                contrib[pl.ds(target * rows + 2 * j + i, 4, stride=4 * rows), :] = block[:4]

    span = 4 * rows
    c_copies = []
    for half in range(2):
        for d in near_last(cross[half]) + [0]:
            to = along_cross(half, d)
            for q, core in ((0, rep), (1, other)):
                start = pl.multiple_of((half * 2 + core) * span, span)
                if d == 0 and q == 0:
                    items[half, pl.ds(pl.multiple_of(rep * span, span), span), :] = contrib[pl.ds(start, span), :]
                    continue
                copy = remote(
                    contrib.at[pl.ds(start, span), :],
                    items.at[half, pl.ds(pl.multiple_of(d * 2 * span + rep * span, span), span), :],
                    c_send.at[half, d, q], c_recv.at[half, d, q], to, core,
                )
                copy.start()
                c_copies.append((half, copy))

    order = near_last(lz) + [0]
    block = 2 * rows
    for half in range(2):
        for h, copy in c_copies:
            if h == half:
                copy.wait_recv()
        slots = side[half] * lz * 2
        for j in range(0, rows, 2):
            value = jnp.concatenate(
                [
                    jnp.concatenate(
                        [items[half, pl.ds(d * 8 * rows + j + i, 8, stride=rows), :] for d in range(cross[half])],
                        axis=0,
                    )
                    for i in range(2)
                ],
                axis=1,
            )
            high = value.astype(BF16)
            low = (value - high.astype(F32)).astype(BF16)
            total = jnp.dot(
                placers[half], jnp.concatenate([high, low], axis=0), preferred_element_type=F32
            )
            for g in range(slots // 8):
                for i in range(2):
                    sums[half, pl.ds(g * 8 * rows + j + i, 8, stride=rows), :] = total[
                        g * 8 : g * 8 + 8, i * LANES : (i + 1) * LANES
                    ]
        for dz in order:
            for d in near_last(side[half]):
                remote(
                    sums.at[half, pl.ds((d * lz + dz) * block, block), :], terms.at[dz, half, d - 1],
                    r_send.at[half, d], r_recv.at[dz], along_side(half, d), rep,
                ).start()

    y_copies = []
    for dz in order:
        pltpu.make_async_copy(terms.at[dz], terms.at[dz], r_recv.at[dz]).wait()
        for half in range(2):
            value = sums[half, pl.ds(dz * block, block), :]
            for d in range(1, side[half]):
                value = value + terms[dz, half, d - 1]
            (parts if dz == 0 else partial)[dz, half] = value
        if dz:
            copy = remote(partial.at[dz], parts.at[dz], y_send.at[dz], y_recv.at[dz], chip(dz=dz), rep)
            copy.start()
            y_copies.append(copy)
    for copy in y_copies:
        copy.wait_recv()
    for half in range(2):
        for cl in range(2):
            value = parts[0, half, pl.ds(cl * rows, rows), :]
            for dz in range(1, lz):
                value = value + parts[dz, half, pl.ds(cl * rows, rows), :]
            out_ref[cl, half] = value

    for copy in list(z_copies.values()) + s_copies + [c for _, c in c_copies] + y_copies:
        copy.wait_send()
    for half in range(2):
        for d in range(1, side[half]):
            whole = pool.at[half, pl.ds(0, lz * 2)]
            pltpu.make_async_copy(whole, whole, d_send.at[half, d]).wait()
            whole = sums.at[half, pl.ds(d * lz * block, lz * block), :]
            pltpu.make_async_copy(whole, whole, r_send.at[half, d]).wait()


def local(dims, current, factors, ranks, pair_clusters):
    lz, ly, lx = dims
    unknowns = current.shape[3]
    rows = unknowns // LANES
    line = max(lx, ly)
    plane = 2 * lz * line
    dma = pltpu.SemaphoreType.DMA
    smem, vmem = pl.BlockSpec(memory_space=pltpu.SMEM), pl.BlockSpec(memory_space=pltpu.VMEM)
    field = pl.pallas_call(
        functools.partial(kernel, dims),
        out_shape=jax.ShapeDtypeStruct((2, 2, rows, LANES), F32),
        in_specs=[smem, smem, vmem, pl.BlockSpec(memory_space=pl.ANY)],
        out_specs=vmem,
        scratch_shapes=[
            pltpu.VMEM((2, plane, rows, LANES), F32),
            pltpu.VMEM((2, line, 2, 4, rows, LANES), F32),
            pltpu.VMEM((2, line, 2, 4, rows, LANES), F32),
            pltpu.VMEM((4, 8 * rows, LANES), F32),
            pltpu.VMEM((4, 4 * RANK_ROWS, unknowns), BF16),
            pltpu.VMEM((4, 8, unknowns), BF16),
            pltpu.VMEM((16 * rows, LANES), F32),
            pltpu.VMEM((2, line * 8 * rows, LANES), F32),
            pltpu.VMEM((2, plane * rows, LANES), F32),
            pltpu.VMEM((lz, 2, line - 1, 2 * rows, LANES), F32),
            pltpu.VMEM((lz, 2, 2 * rows, LANES), F32),
            pltpu.VMEM((lz, 2, 2 * rows, LANES), F32),
            pltpu.VMEM((4, 2, RANK_ROWS, unknowns), F32),
            dma((lz,)), dma((lz,)),
            dma((2, line)), dma((2, line)),
            dma((2, line, 2)), dma((2, line, 2)),
            dma((2, line, 2)), dma((2, line, 2)),
            dma((2, line)), dma((lz,)),
            dma((lz,)), dma((lz,)),
            dma((4,)),
        ],
        compiler_params=pltpu.CompilerParams(
            collective_id=0, has_side_effects=True, vmem_limit_bytes=48 * 1024 * 1024
        ),
    )(pair_clusters.T, ranks, current.reshape(2, 2, rows, LANES), factors)
    return field.reshape(current.shape)


def solution(mesh, dims=(8, 4, 4)):
    placed = (
        P("clu", None, "rep", None),
        P(("clu", "rep"), None, None, None, None),
        P(("clu", "rep")),
        P(),
    )
    return jax.shard_map(
        functools.partial(local, dims), mesh=mesh, in_specs=placed,
        out_specs=P("clu", None, "rep", None), check_vma=False,
    )
```

time: 484 us -> 55.3 us (0.11)
  waiting for transfers between devices: 400 us -> 0 us
  Pallas kernels: 0 us -> 52.4 us
  matrix products: 32.6 us -> 0 us
  local copies, waits for them, and re-layouts: 30.4 us -> 2.72 us
  between operations: 13.9 us -> 0.01 us
    unnamed x5 -> x0, waiting for transfers between devices: 287 us -> none
    all_gather x1 -> x0, waiting for transfers between devices: 113 us -> none  [local(): everything = lax.all_gather(flattened, 'clu', axis=0, tiled=True)]
    pallas_call x0 -> x1, Pallas kernels: none -> 52.4 us  [local(): pl.pallas_call(functools.partial(kernel, dims), out_shape=jax.ShapeDtypeS...]
    dot_general x17 -> x0, matrix products: 32.6 us -> none  [the longest x1 5.6 us: local(): jnp.dot(placer, contributions, precision=high)]
    unnamed x15 -> x7, local copies, waits for them, and re-layouts: 16.5 us -> 2.72 us
  transfers between devices with their start and end apart: 3 -> 0, of which waited for: 3 -> 0; matrix products, arithmetic and copies ran while one was open for 2% -> 0% of each run, Pallas kernels for 0% -> 0%
where the time goes in v1:
time: 55.3 us; the launch traced here: 55.2 us
  Pallas kernels  52.4 us (95%)
  local copies, waits for them, and re-layouts  2.72 us (5%)
    pallas_call x1, Pallas kernels, local(): pl.pallas_call(functools.partial(kernel, dims), out_shape=jax.ShapeDtypeS...  52.4 us
    unnamed x7, local copies, waits for them, and re-layouts  2.72 us

profile of v1, /device:TPU:1, one launch (start us, length us, event | category | flops | bytes accessed | tf_op | source)
XLA Modules:
  0.0 55.2 jit_solution(4202205934516884061)
XLA Ops:
  0.0 0.0 copy-start
  0.0 0.8 %copy-done = f32[2,2,1,2048]{3,2,1,0:T(1,128)S(1)} copy-done((f32[2,2,1,2048]{3,2,1,0:T(1,128)S(1)}, f32[2,2,1,2048]{3,2,1,0:T(1,128)}, u32[]{:S(2)}) %copy-start) | copy-done | bytes 32792
  0.8 0.0 copy-start.1
  0.8 0.7 %copy-done.1 = s32[512,2]{0,1:T(2,128)S(1)} copy-done((s32[512,2]{0,1:T(2,128)S(1)}, s32[512,2]{0,1:T(2,128)}, u32[]{:S(2)}) %copy-start.1) | copy-done | bytes 4120
  1.4 0.0 copy-start.2
  1.4 0.7 %copy-done.2 = s32[2]{0:T(128)S(1)} copy-done((s32[2]{0:T(128)S(1)}, s32[2]{0:T(128)}, u32[]{:S(2)}) %copy-start.2) | copy-done | bytes 32
  2.1 52.4 %shard_map.46 = f32[2,2,16,128]{3,2,1,0:T(8,128)S(1)} custom-call(s32[2,512]{1,0:T(2,128)S(1)} %bitcast.5, s32[2]{0:T(128)S(1)} %copy-done.2, f32[2,2,16,128]{3,2,1,0:T(8,128)S(1)} %bitcast.4, f32[2,2,2,128,2048]{4,3,2,1,0:T(8,128)} %fac_ref.1), custom_call_target="tpu_custom_call" | custom-call | tf_op jit(solution)/shard_map/pallas_call | solution.py:290
  54.6 0.6 %copy.7 = f32[2,2,1,2048]{3,2,1,0:T(1,128)} copy(f32[2,2,1,2048]{3,2,1,0:T(1,128)S(1)} %bitcast.3) | data formatting | bytes 65536
Async XLA Ops:
  0.0 0.8 %copy-start = (f32[2,2,1,2048]{3,2,1,0:T(1,128)S(1)}, f32[2,2,1,2048]{3,2,1,0:T(1,128)}, u32[]{:S(2)}) copy-start(f32[2,2,1,2048]{3,2,1,0:T(1,128)} %param.4) | copy-start | bytes 98308
  0.8 0.7 %copy-start.1 = (s32[512,2]{0,1:T(2,128)S(1)}, s32[512,2]{0,1:T(2,128)}, u32[]{:S(2)}) copy-start(s32[512,2]{0,1:T(2,128)} %param.7) | copy-start | bytes 12292
  1.4 0.7 %copy-start.2 = (s32[2]{0:T(128)S(1)}, s32[2]{0:T(128)}, u32[]{:S(2)}) copy-start(s32[2]{0:T(128)} %ranks_ref.1) | copy-start | bytes 28

commit v2 on v1

v2 whole, which is shorter than its diff:
```python
import functools

import jax
import jax.numpy as jnp
from jax import lax
from jax.experimental import pallas as pl
from jax.experimental.pallas import tpu as pltpu
from jax.sharding import PartitionSpec as P

MESH = pl.DeviceIdType.MESH
LANES = 128
RANK_ROWS = 64
F32, BF16 = jnp.float32, jnp.bfloat16


def near_last(count):
    return sorted(range(1, count), key=lambda d: (-min(d, count - d), d))


def kernel(
    dims, ids_hbm, ranks_hbm, cur_ref, fac_ref, out_ref,
    ids_ref, ranks_ref, slots_ref,
    pool, packed, refs0, refs1, vecs, split, vec8, contrib0, contrib1, items, sums, terms, partial, parts, fac_buf,
    z_send, z_recv, d_send, d_recv, s_send, s_recv, c_send, c_recv, r_send, r_recv, y_send, y_recv, fac_sem, in_sem,
):
    lz, ly, lx = dims
    side = (ly, lx)
    cross = (lx, ly)
    rows = cur_ref.shape[2]
    clu, rep = lax.axis_index("clu"), lax.axis_index("rep")
    other = 1 - rep
    mx, my, mz = lax.rem(clu, lx), lax.rem(lax.div(clu, lx), ly), lax.div(clu, lx * ly)

    def chip(dx=0, dy=0, dz=0):
        x, y, z = lax.rem(mx + dx, lx), lax.rem(my + dy, ly), lax.rem(mz + dz, lz)
        return (z * ly + y) * lx + x

    def along_side(half, d):
        return chip(dy=d % ly) if half == 0 else chip(dx=d % lx)

    def along_cross(half, d):
        return chip(dx=d % lx) if half == 0 else chip(dy=d % ly)

    def ref_id(at, s):
        return ids_ref[s % 2, at * 4 + s // 2]

    def place(cid):
        bx, by = lx.bit_length() - 1, ly.bit_length() - 1
        return (cid >> 1) & (lx - 1), (cid >> (1 + bx)) & (ly - 1), cid >> (1 + bx + by), cid & 1

    def remote(src, dst, ssem, rsem, to, core):
        return pltpu.make_async_remote_copy(
            src_ref=src, dst_ref=dst, send_sem=ssem, recv_sem=rsem, device_id=(to, core), device_id_type=MESH
        )

    barrier = pltpu.get_barrier_semaphore()
    peers = [(clu, other)]
    peers += [(chip(dz=d), rep) for d in range(1, lz)]
    for half in range(2):
        for d in range(1, cross[half]):
            peers += [(along_cross(half, d), rep), (along_cross(half, d), other)]
    for peer in peers:
        pl.semaphore_signal(barrier, inc=1, device_id=peer, device_id_type=MESH)
    own_copies = []
    for half in range(2):
        copy = pltpu.make_async_copy(cur_ref.at[:, half], pool.at[half, pl.ds(0, 2)], in_sem.at[half])
        copy.start()
        own_copies.append(copy)
    table_copies = [
        pltpu.make_async_copy(ids_hbm, ids_ref, in_sem.at[2]), pltpu.make_async_copy(ranks_hbm, ranks_ref, in_sem.at[3])
    ]
    for copy in table_copies:
        copy.start()
    fac_copies = []
    for p in range(2):
        for e in range(2):
            copy = pltpu.make_async_copy(
                fac_ref.at[p, e, :, pl.ds(0, RANK_ROWS), :], fac_buf.at[p * 2 + e], fac_sem.at[p * 2 + e]
            )
            copy.start()
            fac_copies.append(copy)
    for copy in own_copies:
        copy.wait()
    pl.semaphore_wait(barrier, len(peers))

    arrival = near_last(lz)[::-1]
    z_copies = {}
    for d in arrival:
        z_copies[d] = remote(
            pool.at[:, pl.ds(0, 2)], pool.at[:, pl.ds(2 * d, 2)], z_send.at[d], z_recv.at[d], chip(dz=d), rep
        )
        z_copies[d].start()

    def forward(dz):
        for d in near_last(max(side)):
            for half in range(2):
                if d >= side[half]:
                    continue
                remote(
                    pool.at[half, pl.ds(2 * dz, 2)], pool.at[half, pl.ds((d * lz + dz) * 2, 2)],
                    d_send.at[half, d], d_recv.at[half, d], along_side(half, d), rep,
                ).start()

    def split_factor(f):
        fac_copies[f].wait()
        for part in range(2):
            value = fac_buf[f, part]
            high = value.astype(BF16)
            split[f, pl.ds(part * RANK_ROWS, RANK_ROWS), :] = high
            split[f, pl.ds((2 + part) * RANK_ROWS, RANK_ROWS), :] = (value - high.astype(F32)).astype(BF16)

    def find_slots(half):
        for d in range(cross[half]):
            to = along_cross(half, d)
            for s in range(8):
                x, y, z, cl = place(ref_id(to, s))
                shift = (my - y if half == 0 else mx - x) & (side[half] - 1)
                slots_ref[(half * cross[half] + d) * 8 + s] = (shift * lz + ((mz - z) & (lz - 1))) * 2 + cl

    lane = lax.broadcasted_iota(jnp.int32, (8, LANES), 1)

    def make_placer(half):
        target = jnp.full((8, LANES), -1, jnp.int32)
        for d in range(cross[half]):
            source = along_cross(half, cross[half] - d)
            for s in range(8):
                x, y, z, cl = place(ref_id(source, s))
                mine = (x == mx) if half == 0 else (y == my)
                shift = (y - my if half == 0 else x - mx) & (side[half] - 1)
                slot = (shift * lz + ((z - mz) & (lz - 1))) * 2 + cl
                slot = jnp.where(mine, slot, -1)
                at = d * 8 + s
                target = jnp.where((lane == at) | (lane == at + 8 * cross[half]), slot, target)
        slots = side[half] * lz * 2
        wide = jnp.concatenate([target] * (slots // 8), axis=0)[:, : 16 * cross[half]]
        return jnp.where(lax.broadcasted_iota(jnp.int32, wide.shape, 0) == wide, 1.0, 0.0).astype(BF16)

    forward(0)
    for copy in table_copies:
        copy.wait()
    find_slots(0)
    find_slots(1)
    for n, dz in enumerate(arrival):
        z_copies[dz].wait_recv()
        forward(dz)
        if n == 1 % len(arrival):
            split_factor(0)
            split_factor(1)
        if n == 3 % len(arrival):
            split_factor(2)
            split_factor(3)
    placers = [make_placer(0), make_placer(1)]
    for half in range(2):
        for d in range(1, side[half]):
            whole = pool.at[half, pl.ds(d * lz * 2, lz * 2)]
            pltpu.make_async_copy(whole, whole, d_recv.at[half, d]).wait()

    refs = (refs0, refs1)
    s_copies = ([], [])
    for p in range(2):
        for d in near_last(max(cross)) + [0]:
            for half in range(2):
                if d >= cross[half]:
                    continue
                for core in range(2):
                    for s in (2 * p, 2 * p + 1):
                        packed[half, d, core, s] = pool[
                            half, slots_ref[(half * cross[half] + d) * 8 + core * 4 + s]
                        ]
                for q, core in ((0, rep), (1, other)):
                    if d == 0 and q == 0:
                        for s in (2 * p, 2 * p + 1):
                            refs[p][half, 0, rep, s % 2] = packed[half, 0, rep, s]
                        continue
                    copy = remote(
                        packed.at[half, d, core, pl.ds(2 * p, 2)], refs[p].at[half, d, rep],
                        s_send.at[p, half, d, q], s_recv.at[p, half, d, q], along_cross(half, d), core,
                    )
                    copy.start()
                    s_copies[p].append(copy)

    row = lax.broadcasted_iota(jnp.int32, (8, LANES), 0)
    col = lax.broadcasted_iota(jnp.int32, (8, LANES), 1)
    first = row < 4
    sign = jnp.where(lax.rem(row, 4) < 2, -1.0, 1.0).astype(F32)
    span = 4 * rows
    contrib = (contrib0, contrib1)
    c_copies = []
    for p in range(2):
        for copy in s_copies[p]:
            copy.wait_recv()
        for s in (2 * p, 2 * p + 1):
            x, y, z, cl = place(ids_ref[s % 2, clu * 4 + rep * 2 + p])
            dx, dy = (mx - x) & (lx - 1), (my - y) & (ly - 1)
            for k in range(2):
                for half, d in ((0, dx), (1, dy)):
                    value = refs[p][half, d, k, s % 2]
                    vecs[s, pl.ds((half * 2 + k) * rows, rows), :] = value
                    vecs[s, pl.ds((4 + half * 2 + k) * rows, rows), :] = value
        for e in range(2):
            s = 2 * p + e
            for j in range(rows):
                value = vecs[s, pl.ds(j, 8, stride=rows), :]
                high = value.astype(BF16).astype(F32)
                vec8[s, :, pl.ds(j * LANES, LANES)] = jnp.where(first, high, value - high).astype(BF16)
            got = lax.dot_general(
                vec8[s], split[p * 2 + e], (((1,), (1,)), ((), ())), preferred_element_type=F32
            )
            both = got[:, :LANES] + got[:, LANES:]
            both = both + pltpu.roll(both, 4, 0)
            t = both + sign * pltpu.roll(pltpu.roll(both, RANK_ROWS, 1), 2, 0)
            t = jnp.where(col < jnp.minimum(ranks_ref[p], RANK_ROWS), t, 0.0)
            t = t + pltpu.roll(sign * pltpu.roll(t, 2, 0), RANK_ROWS, 1)
            high = t.astype(BF16).astype(F32)
            t = jnp.where(first, high, t - high).astype(BF16)
            t = jnp.concatenate([t, t], axis=1)
            target = 1 - e
            for j in range(rows // 2):
                out = jnp.dot(
                    t, split[p * 2 + 1 - e, :, pl.ds(j * 2 * LANES, 2 * LANES)], preferred_element_type=F32
                )
                for i in range(2):
                    block = out[:, i * LANES : (i + 1) * LANES]
                    block = block + pltpu.roll(block, 4, 0)
                    contrib[p][pl.ds(target * rows + 2 * j + i, 4, stride=2 * rows), :] = block[:4]
        for d in near_last(max(cross)) + [0]:
            for half in range(2):
                if d >= cross[half]:
                    continue
                for q, core in ((0, rep), (1, other)):
                    start = pl.multiple_of((half * 2 + core) * 2 * rows, rows)
                    land = pl.multiple_of((d * 2 + rep) * span + p * 2 * rows, rows)
                    if d == 0 and q == 0:
                        items[half, pl.ds(land, 2 * rows), :] = contrib[p][pl.ds(start, 2 * rows), :]
                        continue
                    copy = remote(
                        contrib[p].at[pl.ds(start, 2 * rows), :], items.at[half, pl.ds(land, 2 * rows), :],
                        c_send.at[p, half, d, q], c_recv.at[p, half, d, q], along_cross(half, d), core,
                    )
                    copy.start()
                    c_copies.append((half, copy))

    order = near_last(lz) + [0]
    block = 2 * rows
    for half in range(2):
        for h, copy in c_copies:
            if h == half:
                copy.wait_recv()
        slots = side[half] * lz * 2
        for j in range(0, rows, 2):
            value = jnp.concatenate(
                [
                    jnp.concatenate(
                        [items[half, pl.ds(d * 8 * rows + j + i, 8, stride=rows), :] for d in range(cross[half])],
                        axis=0,
                    )
                    for i in range(2)
                ],
                axis=1,
            )
            high = value.astype(BF16)
            low = (value - high.astype(F32)).astype(BF16)
            total = jnp.dot(
                placers[half], jnp.concatenate([high, low], axis=0), preferred_element_type=F32
            )
            for g in range(slots // 8):
                for i in range(2):
                    sums[half, pl.ds(g * 8 * rows + j + i, 8, stride=rows), :] = total[
                        g * 8 : g * 8 + 8, i * LANES : (i + 1) * LANES
                    ]
        for dz in order:
            for d in near_last(side[half]):
                remote(
                    sums.at[half, pl.ds((d * lz + dz) * block, block), :], terms.at[dz, half, d - 1],
                    r_send.at[half, d], r_recv.at[dz], along_side(half, d), rep,
                ).start()

    y_copies = []
    for dz in order:
        pltpu.make_async_copy(terms.at[dz], terms.at[dz], r_recv.at[dz]).wait()
        for half in range(2):
            value = sums[half, pl.ds(dz * block, block), :]
            for d in range(1, side[half]):
                value = value + terms[dz, half, d - 1]
            (parts if dz == 0 else partial)[dz, half] = value
        if dz:
            copy = remote(partial.at[dz], parts.at[dz], y_send.at[dz], y_recv.at[dz], chip(dz=dz), rep)
            copy.start()
            y_copies.append(copy)
    for copy in y_copies:
        copy.wait_recv()
    for half in range(2):
        for cl in range(2):
            value = parts[0, half, pl.ds(cl * rows, rows), :]
            for dz in range(1, lz):
                value = value + parts[dz, half, pl.ds(cl * rows, rows), :]
            out_ref[cl, half] = value

    for copy in list(z_copies.values()) + s_copies[0] + s_copies[1] + [c for _, c in c_copies] + y_copies:
        copy.wait_send()
    for half in range(2):
        for d in range(1, side[half]):
            whole = pool.at[half, pl.ds(0, lz * 2)]
            pltpu.make_async_copy(whole, whole, d_send.at[half, d]).wait()
            whole = sums.at[half, pl.ds(d * lz * block, lz * block), :]
            pltpu.make_async_copy(whole, whole, r_send.at[half, d]).wait()


def local(dims, current, factors, ranks, pair_clusters):
    lz, ly, lx = dims
    unknowns = current.shape[3]
    rows = unknowns // LANES
    line = max(lx, ly)
    plane = 2 * lz * line
    dma = pltpu.SemaphoreType.DMA
    field = pl.pallas_call(
        functools.partial(kernel, dims),
        out_shape=jax.ShapeDtypeStruct((2, 2, rows, LANES), F32),
        in_specs=[pl.BlockSpec(memory_space=pltpu.HBM)] * 4,
        out_specs=pl.BlockSpec(memory_space=pltpu.VMEM),
        scratch_shapes=[
            pltpu.SMEM((2, pair_clusters.shape[0]), jnp.int32), pltpu.SMEM(ranks.shape, jnp.int32),
            pltpu.SMEM((16 * line,), jnp.int32),
            pltpu.VMEM((2, plane, rows, LANES), F32),
            pltpu.VMEM((2, line, 2, 4, rows, LANES), F32),
            pltpu.VMEM((2, line, 2, 2, rows, LANES), F32),
            pltpu.VMEM((2, line, 2, 2, rows, LANES), F32),
            pltpu.VMEM((4, 8 * rows, LANES), F32),
            pltpu.VMEM((4, 4 * RANK_ROWS, unknowns), BF16),
            pltpu.VMEM((4, 8, unknowns), BF16),
            pltpu.VMEM((8 * rows, LANES), F32),
            pltpu.VMEM((8 * rows, LANES), F32),
            pltpu.VMEM((2, line * 8 * rows, LANES), F32),
            pltpu.VMEM((2, plane * rows, LANES), F32),
            pltpu.VMEM((lz, 2, line - 1, 2 * rows, LANES), F32),
            pltpu.VMEM((lz, 2, 2 * rows, LANES), F32),
            pltpu.VMEM((lz, 2, 2 * rows, LANES), F32),
            pltpu.VMEM((4, 2, RANK_ROWS, unknowns), F32),
            dma((lz,)), dma((lz,)),
            dma((2, line)), dma((2, line)),
            dma((2, 2, line, 2)), dma((2, 2, line, 2)),
            dma((2, 2, line, 2)), dma((2, 2, line, 2)),
            dma((2, line)), dma((lz,)),
            dma((lz,)), dma((lz,)),
            dma((4,)), dma((4,)),
        ],
        compiler_params=pltpu.CompilerParams(
            collective_id=0, has_side_effects=True, vmem_limit_bytes=48 * 1024 * 1024
        ),
    )(*[
        pltpu.with_memory_space_constraint(operand, pltpu.HBM)
        for operand in (pair_clusters.T, ranks, current.reshape(2, 2, rows, LANES), factors)
    ])
    return field.reshape(current.shape)


def solution(mesh, dims=(8, 4, 4)):
    placed = (
        P("clu", None, "rep", None),
        P(("clu", "rep"), None, None, None, None),
        P(("clu", "rep")),
        P(),
    )
    return jax.shard_map(
        functools.partial(local, dims), mesh=mesh, in_specs=placed,
        out_specs=P("clu", None, "rep", None), check_vma=False,
    )
```

time: 55.3 us -> 49.2 us (0.89)
  Pallas kernels: 52.4 us -> 48.5 us
  local copies, waits for them, and re-layouts: 2.72 us -> 0.62 us
    pallas_call x1, Pallas kernels: 52.4 us -> 48.5 us  [local(): pl.pallas_call(functools.partial(kernel, dims), out_shape=jax.ShapeDtypeS...]
    unnamed x7 -> x1, local copies, waits for them, and re-layouts: 2.72 us -> 0.62 us
where the time goes in v2:
time: 49.2 us; the launch traced here: 49.1 us
  Pallas kernels  48.5 us (99%)
  local copies, waits for them, and re-layouts  0.62 us (1%)
    pallas_call x1, Pallas kernels, local(): pl.pallas_call(functools.partial(kernel, dims), out_shape=jax.ShapeDtypeS...  48.5 us

profile of v2, /device:TPU:1, one launch (start us, length us, event | category | flops | bytes accessed | tf_op | source)
XLA Modules:
  0.0 49.1 jit_solution(10502639772715417195)
XLA Ops:
  0.0 48.5 %shard_map.46 = f32[2,2,16,128]{3,2,1,0:T(8,128)S(1)} custom-call(s32[2,512]{1,0:T(2,128)} %bitcast.5, s32[2]{0:T(128)} %ranks_hbm.1, f32[2,2,16,128]{3,2,1,0:T(8,128)} %bitcast.4, f32[2,2,2,128,2048]{4,3,2,1,0:T(8,128)} %fac_ref.1), custom_call_target="tpu_custom_call" | custom-call | tf_op jit(solution)/shard_map/pallas_call | solution.py:316
  48.5 0.6 %copy.7 = f32[2,2,1,2048]{3,2,1,0:T(1,128)} copy(f32[2,2,1,2048]{3,2,1,0:T(1,128)S(1)} %bitcast.3) | data formatting | bytes 65536

commit v3 on v2

v3 whole, which is shorter than its diff:
```python
import functools

import jax
import jax.numpy as jnp
from jax import lax
from jax.experimental import pallas as pl
from jax.experimental.pallas import tpu as pltpu
from jax.sharding import PartitionSpec as P

MESH = pl.DeviceIdType.MESH
LANES = 128
RANK_ROWS = 48
F32, BF16 = jnp.float32, jnp.bfloat16


def near_last(count):
    return sorted(range(1, count), key=lambda d: (-min(d, count - d), d))


def kernel(
    dims, ids_hbm, ranks_hbm, cur_ref, fac_ref, out_ref,
    ids_ref, ranks_ref, slots_ref,
    pool, packed, refs, vecs, split, vec8, contrib, items, sums, terms, partial, parts, fac_buf,
    z_send, z_recv, d_send, d_recv, s_send, s_recv, c_send, c_recv, r_send, r_recv, y_send, y_recv, fac_sem, in_sem,
):
    lz, ly, lx = dims
    side = (ly, lx)
    cross = (lx, ly)
    rows = cur_ref.shape[2]
    line = lx
    clu, rep = lax.axis_index("clu"), lax.axis_index("rep")
    other = 1 - rep
    mx, my, mz = lax.rem(clu, lx), lax.rem(lax.div(clu, lx), ly), lax.div(clu, lx * ly)

    def chip(dx=0, dy=0, dz=0):
        x, y, z = lax.rem(mx + dx, lx), lax.rem(my + dy, ly), lax.rem(mz + dz, lz)
        return (z * ly + y) * lx + x

    def along_side(half, d):
        return chip(dy=d % ly) if half == 0 else chip(dx=d % lx)

    def along_cross(half, d):
        return chip(dx=d % lx) if half == 0 else chip(dy=d % ly)

    def ref_id(at, s):
        return ids_ref[s % 2, at * 4 + s // 2]

    def place(cid):
        bx, by = lx.bit_length() - 1, ly.bit_length() - 1
        return (cid >> 1) & (lx - 1), (cid >> (1 + bx)) & (ly - 1), cid >> (1 + bx + by), cid & 1

    def drain(ref, sem):
        pltpu.make_async_copy(ref, ref, sem).wait()

    def remote(src, dst, ssem, rsem, to, core):
        return pltpu.make_async_remote_copy(
            src_ref=src, dst_ref=dst, send_sem=ssem, recv_sem=rsem, device_id=(to, core), device_id_type=MESH
        )

    direct = [d for d in range(1, lz) if min(d, lz - d) <= 2]
    relays = [(3, 2, 1, (0, 1)), (5, 6, 7, (0, 1)), (4, 2, 2, (0,)), (4, 6, 6, (1,))] if lz == 8 else []
    barrier = pltpu.get_barrier_semaphore()
    peers = [(clu, other)]
    peers += [(chip(dz=d), rep) for d in direct]
    for half in range(2):
        for d in range(1, cross[half]):
            peers += [(along_cross(half, d), rep), (along_cross(half, d), other)]
    for peer in peers:
        pl.semaphore_signal(barrier, inc=1, device_id=peer, device_id_type=MESH)
    for half in range(2):
        pltpu.make_async_copy(cur_ref.at[:, half], pool.at[half, pl.ds(0, 2)], in_sem.at[0]).start()
    table_copies = [
        pltpu.make_async_copy(ids_hbm, ids_ref, in_sem.at[1]), pltpu.make_async_copy(ranks_hbm, ranks_ref, in_sem.at[2])
    ]
    for copy in table_copies:
        copy.start()
    fac_copies = []
    for p in range(2):
        for e in range(2):
            copy = pltpu.make_async_copy(
                fac_ref.at[p, e, :, pl.ds(0, RANK_ROWS), :], fac_buf.at[p * 2 + e], fac_sem.at[p * 2 + e]
            )
            copy.start()
            fac_copies.append(copy)
    drain(pool.at[:, pl.ds(0, 2)], in_sem.at[0])
    pl.semaphore_wait(barrier, len(peers))

    arrivals = {}

    def send_along_z(held, lands, step, halves, n):
        part = pl.ds(halves[0], len(halves))
        copy = remote(
            pool.at[part, pl.ds(2 * held, 2)], pool.at[part, pl.ds(2 * lands, 2)],
            z_send, z_recv.at[n], chip(dz=step), rep,
        )
        copy.start()
        arrivals.setdefault(lands, []).append(copy)

    arrival = [d for d in near_last(lz) if d in direct]
    for n, d in enumerate(arrival):
        send_along_z(0, d, d, (0, 1), n)
    arrival += [d for d in (3, 5, 4) if d not in direct and d < lz]

    def forward(dz):
        for d in near_last(max(side)):
            for half in range(2):
                if d >= side[half]:
                    continue
                remote(
                    pool.at[half, pl.ds(2 * dz, 2)], pool.at[half, pl.ds((d * lz + dz) * 2, 2)],
                    d_send, d_recv, along_side(half, d), rep,
                ).start()

    def split_factor(f):
        fac_copies[f].wait()
        for part in range(2):
            value = fac_buf[f, part]
            high = value.astype(BF16)
            split[f, 0, pl.ds(part * RANK_ROWS, RANK_ROWS), :] = high
            split[f, 1, pl.ds(part * RANK_ROWS, RANK_ROWS), :] = (value - high.astype(F32)).astype(BF16)

    def find_slots(half):
        for d in range(cross[half]):
            to = along_cross(half, d)
            for s in range(8):
                x, y, z, cl = place(ref_id(to, s))
                shift = (my - y if half == 0 else mx - x) & (side[half] - 1)
                slots_ref[(half * cross[half] + d) * 8 + s] = (shift * lz + ((mz - z) & (lz - 1))) * 2 + cl

    lane = lax.broadcasted_iota(jnp.int32, (8, LANES), 1)

    def make_placer(half):
        target = jnp.full((8, LANES), -1, jnp.int32)
        for d in range(cross[half]):
            source = along_cross(half, cross[half] - d)
            for s in range(8):
                x, y, z, cl = place(ref_id(source, s))
                mine = (x == mx) if half == 0 else (y == my)
                shift = (y - my if half == 0 else x - mx) & (side[half] - 1)
                slot = (shift * lz + ((z - mz) & (lz - 1))) * 2 + cl
                slot = jnp.where(mine, slot, -1)
                at = d * 8 + s
                target = jnp.where((lane == at) | (lane == at + 8 * cross[half]), slot, target)
        slots = side[half] * lz * 2
        wide = jnp.concatenate([target] * (slots // 8), axis=0)[:, : 16 * cross[half]]
        return jnp.where(lax.broadcasted_iota(jnp.int32, wide.shape, 0) == wide, 1.0, 0.0).astype(BF16)

    forward(0)
    for copy in table_copies:
        copy.wait()
    find_slots(0)
    find_slots(1)
    for n, dz in enumerate(arrival):
        for copy in arrivals[dz]:
            copy.wait_recv()
        for m, (lands, held, step, halves) in enumerate(relays):
            if held == dz:
                send_along_z(held, lands, step, halves, len(direct) + m)
        forward(dz)
        if n == 1 % len(arrival):
            split_factor(0)
            split_factor(1)
        if n == 3 % len(arrival):
            split_factor(2)
            split_factor(3)
    placers = [make_placer(0), make_placer(1)]
    drain(pool.at[:, pl.ds(2 * lz, 2 * lz * (line - 1))], d_recv)

    for s in range(4):
        for d in near_last(max(cross)) + [0]:
            for half in range(2):
                if d >= cross[half]:
                    continue
                for core in range(2):
                    packed[half, d, core, s] = pool[half, slots_ref[(half * cross[half] + d) * 8 + core * 4 + s]]
                for q, core in ((0, rep), (1, other)):
                    if d == 0 and q == 0:
                        refs[s][half, 0, rep] = packed[half, 0, rep, s]
                        continue
                    remote(
                        packed.at[half, d, core, s], refs[s].at[half, d, rep],
                        s_send, s_recv.at[s, min(d, 1)], along_cross(half, d), core,
                    ).start()

    row = lax.broadcasted_iota(jnp.int32, (8, LANES), 0)
    col = lax.broadcasted_iota(jnp.int32, (8, LANES), 1)
    first = row < 4
    sign = jnp.where(lax.rem(row, 4) < 2, -1.0, 1.0).astype(F32)
    for s in range(4):
        p, e = s // 2, s % 2
        x, y, z, cl = place(ids_ref[e, clu * 4 + rep * 2 + p])
        dx, dy = (mx - x) & (lx - 1), (my - y) & (ly - 1)
        drain(refs[s].at[:, pl.ds(1, line - 1)], s_recv.at[s, 1])
        drain(refs[s].at[:, 0, other], s_recv.at[s, 0])
        for k in range(2):
            for half, d in ((0, dx), (1, dy)):
                value = refs[s][half, d, k]
                vecs[s, pl.ds((half * 2 + k) * rows, rows), :] = value
                vecs[s, pl.ds((4 + half * 2 + k) * rows, rows), :] = value
        for j in range(rows):
            value = vecs[s, pl.ds(j, 8, stride=rows), :]
            high = value.astype(BF16).astype(F32)
            vec8[s, :, pl.ds(j * LANES, LANES)] = jnp.where(first, high, value - high).astype(BF16)
        both = sum(
            lax.dot_general(vec8[s], split[s, part], (((1,), (1,)), ((), ())), preferred_element_type=F32)
            for part in range(2)
        )
        both = jnp.concatenate([both, jnp.zeros((8, LANES - 2 * RANK_ROWS), F32)], axis=1)
        both = both + pltpu.roll(both, 4, 0)
        t = both + sign * pltpu.roll(pltpu.roll(both, LANES - RANK_ROWS, 1), 2, 0)
        t = jnp.where(col < jnp.minimum(ranks_ref[p], RANK_ROWS), t, 0.0)
        t = t + pltpu.roll(sign * pltpu.roll(t, 2, 0), RANK_ROWS, 1)
        high = t.astype(BF16).astype(F32)
        t = jnp.where(first, high, t - high).astype(BF16)[:, : 2 * RANK_ROWS]
        target = 2 * p + 1 - e
        for j in range(rows // 2):
            out = sum(
                jnp.dot(t, split[target, part, :, pl.ds(j * 2 * LANES, 2 * LANES)], preferred_element_type=F32)
                for part in range(2)
            )
            for i in range(2):
                block = out[:, i * LANES : (i + 1) * LANES]
                block = block + pltpu.roll(block, 4, 0)
                contrib[s][pl.ds(2 * j + i, 4, stride=rows), :] = block[:4]
        for d in near_last(max(cross)) + [0]:
            for half in range(2):
                if d >= cross[half]:
                    continue
                for q, core in ((0, rep), (1, other)):
                    start = pl.multiple_of((half * 2 + core) * rows, rows)
                    land = pl.multiple_of(((d * 2 + rep) * 4 + target) * rows, rows)
                    if d == 0 and q == 0:
                        items[half, pl.ds(land, rows), :] = contrib[s][pl.ds(start, rows), :]
                        continue
                    remote(
                        contrib[s].at[pl.ds(start, rows), :], items.at[half, pl.ds(land, rows), :],
                        c_send, c_recv.at[half, min(d, 1)], along_cross(half, d), core,
                    ).start()

    order = near_last(lz) + [0]
    block = 2 * rows
    for half in range(2):
        drain(items.at[half, pl.ds(8 * rows, 8 * rows * (line - 1)), :], c_recv.at[half, 1])
        drain(items.at[half, pl.ds(pl.multiple_of(other * 4 * rows, rows), 4 * rows), :], c_recv.at[half, 0])
        slots = side[half] * lz * 2
        for j in range(0, rows, 2):
            value = jnp.concatenate(
                [
                    jnp.concatenate(
                        [items[half, pl.ds(d * 8 * rows + j + i, 8, stride=rows), :] for d in range(cross[half])],
                        axis=0,
                    )
                    for i in range(2)
                ],
                axis=1,
            )
            high = value.astype(BF16)
            low = (value - high.astype(F32)).astype(BF16)
            total = jnp.dot(
                placers[half], jnp.concatenate([high, low], axis=0), preferred_element_type=F32
            )
            for g in range(slots // 8):
                for i in range(2):
                    sums[half, pl.ds(g * 8 * rows + j + i, 8, stride=rows), :] = total[
                        g * 8 : g * 8 + 8, i * LANES : (i + 1) * LANES
                    ]
        for dz in order:
            for d in near_last(side[half]):
                remote(
                    sums.at[half, pl.ds((d * lz + dz) * block, block), :], terms.at[dz, half, d - 1],
                    r_send, r_recv.at[dz], along_side(half, d), rep,
                ).start()

    for dz in order:
        drain(terms.at[dz], r_recv.at[dz])
        for half in range(2):
            value = sums[half, pl.ds(dz * block, block), :]
            for d in range(1, side[half]):
                value = value + terms[dz, half, d - 1]
            (parts if dz == 0 else partial)[dz, half] = value
        if dz:
            remote(partial.at[dz], parts.at[dz], y_send, y_recv, chip(dz=dz), rep).start()
    drain(parts.at[pl.ds(1, lz - 1)], y_recv)
    for half in range(2):
        for cl in range(2):
            value = parts[0, half, pl.ds(cl * rows, rows), :]
            for dz in range(1, lz):
                value = value + parts[dz, half, pl.ds(cl * rows, rows), :]
            out_ref[cl, half] = value

    drain(pool.at[:, pl.ds(2, 2 * lz - 2)], z_send)
    drain(pool.at[:, pl.ds(2 * lz, 2 * lz * (line - 1))], d_send)
    drain(pool.at[:, pl.ds(0, 4 * (2 * line - 1))], s_send)
    drain(pool.at[:, pl.ds(0, 4 * (2 * line - 1))], c_send)
    drain(sums.at[:, pl.ds(lz * block, lz * block * (line - 1)), :], r_send)
    drain(parts.at[pl.ds(1, lz - 1)], y_send)


def local(dims, current, factors, ranks, pair_clusters):
    lz, ly, lx = dims
    unknowns = current.shape[3]
    rows = unknowns // LANES
    line = max(lx, ly)
    plane = 2 * lz * line
    dma = pltpu.SemaphoreType.DMA
    field = pl.pallas_call(
        functools.partial(kernel, dims),
        out_shape=jax.ShapeDtypeStruct((2, 2, rows, LANES), F32),
        in_specs=[pl.BlockSpec(memory_space=pltpu.HBM)] * 4,
        out_specs=pl.BlockSpec(memory_space=pltpu.VMEM),
        scratch_shapes=[
            pltpu.SMEM((2, pair_clusters.shape[0]), jnp.int32), pltpu.SMEM(ranks.shape, jnp.int32),
            pltpu.SMEM((16 * line,), jnp.int32),
            pltpu.VMEM((2, plane, rows, LANES), F32),
            pltpu.VMEM((2, line, 2, 4, rows, LANES), F32),
            [pltpu.VMEM((2, line, 2, rows, LANES), F32)] * 4,
            pltpu.VMEM((4, 8 * rows, LANES), F32),
            pltpu.VMEM((4, 2, 2 * RANK_ROWS, unknowns), BF16),
            pltpu.VMEM((4, 8, unknowns), BF16),
            [pltpu.VMEM((4 * rows, LANES), F32)] * 4,
            pltpu.VMEM((2, line * 8 * rows, LANES), F32),
            pltpu.VMEM((2, plane * rows, LANES), F32),
            pltpu.VMEM((lz, 2, line - 1, 2 * rows, LANES), F32),
            pltpu.VMEM((lz, 2, 2 * rows, LANES), F32),
            pltpu.VMEM((lz, 2, 2 * rows, LANES), F32),
            pltpu.VMEM((4, 2, RANK_ROWS, unknowns), F32),
            dma, dma((lz,)), dma, dma, dma, dma((4, 2)), dma, dma((2, 2)), dma, dma((lz,)), dma, dma,
            dma((4,)), dma((3,)),
        ],
        compiler_params=pltpu.CompilerParams(
            collective_id=0, has_side_effects=True, vmem_limit_bytes=48 * 1024 * 1024
        ),
    )(*[
        pltpu.with_memory_space_constraint(operand, pltpu.HBM)
        for operand in (pair_clusters.T, ranks, current.reshape(2, 2, rows, LANES), factors)
    ])
    return field.reshape(current.shape)


def solution(mesh, dims=(8, 4, 4)):
    placed = (
        P("clu", None, "rep", None),
        P(("clu", "rep"), None, None, None, None),
        P(("clu", "rep")),
        P(),
    )
    return jax.shard_map(
        functools.partial(local, dims), mesh=mesh, in_specs=placed,
        out_specs=P("clu", None, "rep", None), check_vma=False,
    )
```

time: 49.2 us -> 45.3 us (0.921)
  Pallas kernels: 48.5 us -> 44.6 us
    pallas_call x1, Pallas kernels: 48.5 us -> 44.6 us  [local(): pl.pallas_call(functools.partial(kernel, dims), out_shape=jax.ShapeDtypeS...]
where the time goes in v3:
time: 45.3 us
  Pallas kernels  44.6 us (98%)
  local copies, waits for them, and re-layouts  0.62 us (1%)
    pallas_call x1, Pallas kernels, local(): pl.pallas_call(functools.partial(kernel, dims), out_shape=jax.ShapeDtypeS...  44.6 us

profile of v3, /device:TPU:1, one launch (start us, length us, event | category | flops | bytes accessed | tf_op | source)
XLA Modules:
  0.0 45.3 jit_solution(1333399336509227735)
XLA Ops:
  0.0 44.6 %shard_map.46 = f32[2,2,16,128]{3,2,1,0:T(8,128)S(1)} custom-call(s32[2,512]{1,0:T(2,128)} %bitcast.5, s32[2]{0:T(128)} %ranks_hbm.1, f32[2,2,16,128]{3,2,1,0:T(8,128)} %bitcast.4, f32[2,2,2,128,2048]{4,3,2,1,0:T(8,128)} %fac_ref.1), custom_call_target="tpu_custom_call" | custom-call | tf_op jit(solution)/shard_map/pallas_call | solution.py:306
  44.6 0.6 %copy.7 = f32[2,2,1,2048]{3,2,1,0:T(1,128)} copy(f32[2,2,1,2048]{3,2,1,0:T(1,128)S(1)} %bitcast.3) | data formatting | bytes 65536

commit v4 on v3

--- a/solution.py
+++ b/solution.py
@@ -186,12 +186,10 @@
     col = lax.broadcasted_iota(jnp.int32, (8, LANES), 1)
     first = row < 4
     sign = jnp.where(lax.rem(row, 4) < 2, -1.0, 1.0).astype(F32)
-    for s in range(4):
+    def project(s):
         p, e = s // 2, s % 2
         x, y, z, cl = place(ids_ref[e, clu * 4 + rep * 2 + p])
         dx, dy = (mx - x) & (lx - 1), (my - y) & (ly - 1)
-        drain(refs[s].at[:, pl.ds(1, line - 1)], s_recv.at[s, 1])
-        drain(refs[s].at[:, 0, other], s_recv.at[s, 0])
         for k in range(2):
             for half, d in ((0, dx), (1, dy)):
                 value = refs[s][half, d, k]
@@ -211,8 +209,10 @@
         t = jnp.where(col < jnp.minimum(ranks_ref[p], RANK_ROWS), t, 0.0)
         t = t + pltpu.roll(sign * pltpu.roll(t, 2, 0), RANK_ROWS, 1)
         high = t.astype(BF16).astype(F32)
-        t = jnp.where(first, high, t - high).astype(BF16)[:, : 2 * RANK_ROWS]
-        target = 2 * p + 1 - e
+        return jnp.where(first, high, t - high).astype(BF16)[:, : 2 * RANK_ROWS]
+
+    def expand(s, t):
+        target = s ^ 1
         for j in range(rows // 2):
             out = sum(
                 jnp.dot(t, split[target, part, :, pl.ds(j * 2 * LANES, 2 * LANES)], preferred_element_type=F32)
@@ -222,6 +222,9 @@
                 block = out[:, i * LANES : (i + 1) * LANES]
                 block = block + pltpu.roll(block, 4, 0)
                 contrib[s][pl.ds(2 * j + i, 4, stride=rows), :] = block[:4]
+
+    def send_back(s):
+        target = s ^ 1
         for d in near_last(max(cross)) + [0]:
             for half in range(2):
                 if d >= cross[half]:
@@ -236,6 +239,16 @@
                         contrib[s].at[pl.ds(start, rows), :], items.at[half, pl.ds(land, rows), :],
                         c_send, c_recv.at[half, min(d, 1)], along_cross(half, d), core,
                     ).start()
+
+    projected = {}
+    for s in range(5):
+        if s < 4:
+            drain(refs[s].at[:, pl.ds(1, line - 1)], s_recv.at[s, 1])
+            drain(refs[s].at[:, 0, other], s_recv.at[s, 0])
+            projected[s] = project(s)
+        if s > 0:
+            expand(s - 1, projected[s - 1])
+            send_back(s - 1)
 
     order = near_last(lz) + [0]
     block = 2 * rows

time: 45.3 us -> 44.7 us (0.987)
  Pallas kernels: 44.6 us -> 44 us
    pallas_call x1, Pallas kernels: 44.6 us -> 44 us  [local(): pl.pallas_call(functools.partial(kernel, dims), out_shape=jax.ShapeDtypeS...]
where the time goes in v4:
time: 44.7 us; the launch traced here: 44.6 us
  Pallas kernels  44 us (98%)
  local copies, waits for them, and re-layouts  0.62 us (1%)
    pallas_call x1, Pallas kernels, local(): pl.pallas_call(functools.partial(kernel, dims), out_shape=jax.ShapeDtypeS...  44 us

profile of v4, /device:TPU:1, one launch (start us, length us, event | category | flops | bytes accessed | tf_op | source)
XLA Modules:
  0.0 44.6 jit_solution(7463122811692827743)
XLA Ops:
  0.0 44.0 %shard_map.46 = f32[2,2,16,128]{3,2,1,0:T(8,128)S(1)} custom-call(s32[2,512]{1,0:T(2,128)} %bitcast.5, s32[2]{0:T(128)} %ranks_hbm.1, f32[2,2,16,128]{3,2,1,0:T(8,128)} %bitcast.4, f32[2,2,2,128,2048]{4,3,2,1,0:T(8,128)} %fac_ref.1), custom_call_target="tpu_custom_call" | custom-call | tf_op jit(solution)/shard_map/pallas_call | solution.py:319
  44.0 0.6 %copy.7 = f32[2,2,1,2048]{3,2,1,0:T(1,128)} copy(f32[2,2,1,2048]{3,2,1,0:T(1,128)S(1)} %bitcast.3) | data formatting | bytes 65536

commit v5 on v4

--- a/solution.py
+++ b/solution.py
@@ -252,6 +252,14 @@
 
     order = near_last(lz) + [0]
     block = 2 * rows
+
+    def send_sums(half, dz):
+        for d in near_last(line):
+            remote(
+                sums.at[half, pl.ds((d * lz + dz) * block, block), :], terms.at[dz, half, d - 1],
+                r_send, r_recv.at[dz], along_side(half, d), rep,
+            ).start()
+
     for half in range(2):
         drain(items.at[half, pl.ds(8 * rows, 8 * rows * (line - 1)), :], c_recv.at[half, 1])
         drain(items.at[half, pl.ds(pl.multiple_of(other * 4 * rows, rows), 4 * rows), :], c_recv.at[half, 0])
@@ -277,12 +285,14 @@
                     sums[half, pl.ds(g * 8 * rows + j + i, 8, stride=rows), :] = total[
                         g * 8 : g * 8 + 8, i * LANES : (i + 1) * LANES
                     ]
-        for dz in order:
-            for d in near_last(side[half]):
-                remote(
-                    sums.at[half, pl.ds((d * lz + dz) * block, block), :], terms.at[dz, half, d - 1],
-                    r_send, r_recv.at[dz], along_side(half, d), rep,
-                ).start()
+        if half == 0:
+            for dz in order[:2]:
+                send_sums(half, dz)
+    for dz in order[:2]:
+        send_sums(1, dz)
+    for dz in order[2:]:
+        send_sums(0, dz)
+        send_sums(1, dz)
 
     for dz in order:
         drain(terms.at[dz], r_recv.at[dz])

time: 44.7 us -> 44.6 us (level)
  no operation moved by 1% of the time
where the time goes in v5:
time: 44.6 us
  Pallas kernels  43.9 us (98%)
  local copies, waits for them, and re-layouts  0.62 us (1%)
    pallas_call x1, Pallas kernels, local(): pl.pallas_call(functools.partial(kernel, dims), out_shape=jax.ShapeDtypeS...  43.9 us

profile of v5, /device:TPU:1, one launch (start us, length us, event | category | flops | bytes accessed | tf_op | source)
XLA Modules:
  0.0 44.6 jit_solution(223391259015409221)
XLA Ops:
  0.0 43.9 %shard_map.46 = f32[2,2,16,128]{3,2,1,0:T(8,128)S(1)} custom-call(s32[2,512]{1,0:T(2,128)} %bitcast.5, s32[2]{0:T(128)} %ranks_hbm.1, f32[2,2,16,128]{3,2,1,0:T(8,128)} %bitcast.4, f32[2,2,2,128,2048]{4,3,2,1,0:T(8,128)} %fac_ref.1), custom_call_target="tpu_custom_call" | custom-call | tf_op jit(solution)/shard_map/pallas_call | solution.py:329
  44.0 0.6 %copy.7 = f32[2,2,1,2048]{3,2,1,0:T(1,128)} copy(f32[2,2,1,2048]{3,2,1,0:T(1,128)S(1)} %bitcast.3) | data formatting | bytes 65536
